TPU v7x, 32 devices: a whole 2x2x4 slice. The times are simulated.
32 devices in a mesh: dp: 2 (over x), ctx: 16 (over z, y, core).
Axes of the slice: x: 2, y: 2, z: 4, core: 2. Of those that a mesh axis runs over, the one named last changes fastest.
Arguments:
- features: bfloat16 [2, 2048, 1536], P('dp', 'ctx'), may hold values from -500 to 500
- gain: float32 [1536], replicated, may hold values from 0.1 to 1.9
- conv_weight: bfloat16 [5, 1536, 768], replicated, may hold values from -0.0625 to 0.0625
- cotangent: bfloat16 [2, 2048, 768], P('dp', 'ctx'), may hold values from -15 to 15
Outputs:
- convolved: bfloat16 [2, 2048, 768], P('dp', 'ctx')
- input_grad: bfloat16 [2, 2048, 1536], P('dp', 'ctx')
- gain_grad: float32 [1536], replicated
All inputs are finite; a program needn't handle non-finite values.
Results may differ from a plain program's by a relative error of at most 0.0054.
Values may be sent and summed in bfloat16 or wider, within the bound.
A program may use at most 64 MiB of HBM per device.

v0:
```python
import math
import jax
import jax.numpy as jnp
from jax import lax
from jax.sharding import PartitionSpec as P

KERNEL_TAPS = 5
EPS = 1e-06


def shifted(block, axis, distance):
    devices = range(lax.axis_size(axis))
    route = [(i - distance, i) for i in devices if i - distance in devices]
    return lax.ppermute(block, axis, route)


def activate(values):
    return jax.nn.gelu(values, approximate=True)


def flip_channels(values):
    return values[:, :, ::-1]


def taps_ahead(values, shard_hops):
    pieces = []
    for tap_index in range(KERNEL_TAPS):
        if tap_index == KERNEL_TAPS // 2:
            pieces.append(values)
        else:
            pieces.append(shifted(values, "ctx", -(tap_index - KERNEL_TAPS // 2) * shard_hops))
    return pieces


def taps_behind(values, shard_hops):
    pieces = []
    for tap_index in range(KERNEL_TAPS):
        if tap_index == KERNEL_TAPS // 2:
            pieces.append(values)
        else:
            pieces.append(shifted(values, "ctx", (tap_index - KERNEL_TAPS // 2) * shard_hops))
    return pieces


def apply_forward(pieces, weight):
    lead = pieces[0].shape[0]
    middle = pieces[0].shape[1]
    total = jnp.zeros((lead * middle, weight.shape[2]), jnp.float32)
    for tap_index in range(KERNEL_TAPS):
        flat_rows = pieces[tap_index].reshape(lead * middle, pieces[tap_index].shape[2])
        total = total + jnp.dot(flat_rows, weight[tap_index], preferred_element_type=jnp.float32)
    return total.reshape(lead, middle, weight.shape[2])


def apply_backward(pieces, weight):
    lead = pieces[0].shape[0]
    middle = pieces[0].shape[1]
    total = jnp.zeros((lead * middle, weight.shape[1]), jnp.float32)
    for tap_index in range(KERNEL_TAPS):
        flat_rows = pieces[tap_index].reshape(lead * middle, pieces[tap_index].shape[2])
        total = total + lax.dot_general(
            flat_rows,
            weight[tap_index],
            (((1,), (1,)), ((), ())),
            preferred_element_type=jnp.float32,
        )
    return total.reshape(lead, middle, weight.shape[1])


def per_device(features, gain, conv_weight, cotangent):
    shard_hops = lax.axis_size("ctx") // 8
    wide = features.astype(jnp.float32)
    inv_rms = lax.rsqrt(jnp.mean(wide * wide, axis=-1, keepdims=True) + EPS)
    normed = wide * inv_rms
    scaled = normed * gain
    hidden = activate(scaled).astype(jnp.bfloat16)
    ahead = taps_ahead(hidden, shard_hops)
    forward_term = apply_forward(ahead, conv_weight)
    flipped = [
        flip_channels(ahead[KERNEL_TAPS - 1 - tap_index]) for tap_index in range(KERNEL_TAPS)
    ]
    reverse_term = flip_channels(apply_forward(flipped, conv_weight).astype(jnp.bfloat16))
    convolved = (forward_term + reverse_term.astype(jnp.float32)).astype(jnp.bfloat16)
    behind = taps_behind(cotangent, shard_hops)
    back_forward = apply_backward(behind, conv_weight)
    flipped_grads = [
        flip_channels(behind[KERNEL_TAPS - 1 - tap_index]) for tap_index in range(KERNEL_TAPS)
    ]
    back_reverse = flip_channels(apply_backward(flipped_grads, conv_weight).astype(jnp.bfloat16))
    grad_hidden = back_forward + back_reverse.astype(jnp.float32)
    _, pullback = jax.vjp(activate, scaled)
    grad_scaled = pullback(grad_hidden)[0]
    partial_sum = jnp.sum(grad_scaled * normed, axis=(0, 1))
    summed = lax.psum(partial_sum, ("dp", "ctx"))
    total_rows = features.shape[0] * features.shape[1] * lax.axis_size("dp") * lax.axis_size("ctx")
    gain_grad = summed / math.sqrt(total_rows)
    grad_normed = grad_scaled * gain
    spread_term = jnp.mean(grad_normed * normed, axis=-1, keepdims=True)
    input_grad = (inv_rms * (grad_normed - normed * spread_term)).astype(jnp.bfloat16)
    return (convolved, input_grad, gain_grad)


def solution(mesh):
    return jax.shard_map(
        per_device,
        mesh=mesh,
        in_specs=(P("dp", "ctx", None), P(), P(), P("dp", "ctx", None)),
        out_specs=(P("dp", "ctx", None), P("dp", "ctx", None), P()),
        check_vma=False,
    )
```

profile of v0, /device:TPU:0, one launch (start us, length us, event | category | flops | bytes accessed | tf_op | source)
XLA Modules:
  0.0 152.5 jit_solution(12865565920787407074)
XLA Ops:
  0.6 4.9 %collective-permute-start.6 = (bf16[1,128,768]{2,1,0:T(8,128)(2,1)}, bf16[1,128,768]{2,1,0:T(8,128)(2,1)S(1)}, u32[]{:S(2)}, u32[]{:S(2)}) collective-permute-start(bf16[1,128,768]{2,1,0:T(8,128)(2,1)} %param.7), channel_id=1, source_target_pairs={{0,2},{1,3},{2,4},{3,5},{4,6},{5,7},{6,8},{7,9},{8,10},{9,11},{10,... | collective-permute-start | bytes 589832 | tf_op jit(solution)/shard_map/ppermute | solution.py:14
  5.5 3.5 %collective-permute-start.7 = (bf16[1,128,768]{2,1,0:T(8,128)(2,1)}, bf16[1,128,768]{2,1,0:T(8,128)(2,1)S(1)}, u32[]{:S(2)}, u32[]{:S(2)}) collective-permute-start(bf16[1,128,768]{2,1,0:T(8,128)(2,1)} %param.7), channel_id=1, source_target_pairs={{0,4},{1,5},{2,6},{3,7},{4,8},{5,9},{6,10},{7,11},{8,12},{9,13},{1... | collective-permute-start | bytes 589832 | tf_op jit(solution)/shard_map/ppermute | solution.py:14
  9.0 1.3 collective-permute-start.4
  10.3 1.3 collective-permute-start.5
  11.6 2.7 %rev.39 = bf16[1,128,768]{2,1,0:T(8,128)(2,1)S(1)} reverse(bf16[1,128,768]{2,1,0:T(8,128)(2,1)} %param.7), dimensions={2} | reverse | bytes 393216 | tf_op jit(solution)/shard_map/rev | solution.py:22
  14.3 2.7 %fusion.23 = f32[128,1536]{1,0:T(8,128)S(1)} fusion(bf16[5,1536,768]{2,1,0:T(8,128)(2,1)} %param.6, bf16[1,128,768]{2,1,0:T(8,128)(2,1)} %param.7), kind=kOutput, calls=%fused_computation.27 | convolution fusion | flops 301989888 | bytes 3342336 | tf_op jit(solution)/shard_map/dot_general | solution.py:61
  17.0 2.6 %fusion.21 = f32[128,1536]{1,0:T(8,128)S(1)} fusion(bf16[5,1536,768]{2,1,0:T(8,128)(2,1)} %param.6, bf16[1,128,768]{2,1,0:T(8,128)(2,1)S(1)} %rev.39), kind=kOutput, calls=%fused_computation.25 | convolution fusion | flops 301989888 | bytes 3342336 | tf_op jit(solution)/shard_map/dot_general | solution.py:61
  19.5 1.2 fusion.116
  20.7 0.0 collective-permute-done.6
  20.7 0.0 copy-start.3
  20.7 0.6 rev.38
  21.4 2.5 %fusion.29 = f32[128,1536]{1,0:T(8,128)S(1)} fusion(bf16[5,1536,768]{2,1,0:T(8,128)(2,1)} %param.6, bf16[1,128,768]{2,1,0:T(8,128)(2,1)S(1)} %rev.38), kind=kOutput, calls=%fused_computation.33 | convolution fusion | flops 301989888 | bytes 3342336 | tf_op jit(solution)/shard_map/dot_general | solution.py:61
  23.9 0.0 collective-permute-done.7
  23.9 0.0 copy-done.3
  23.9 0.0 copy-start.1
  24.0 0.7 copy-done.1
  24.6 2.2 %rev.37 = bf16[1,128,768]{2,1,0:T(8,128)(2,1)} reverse(bf16[1,128,768]{2,1,0:T(8,128)(2,1)S(1)} %collective-permute-done.7), dimensions={2} | reverse | bytes 393216 | tf_op jit(solution)/shard_map/rev | solution.py:22
  26.8 0.0 copy-start
  26.8 0.0 copy-start.5
  26.8 2.7 %fusion.1 = f32[128,1536]{1,0:T(8,128)S(1)} fusion(f32[128,1536]{1,0:T(8,128)S(1)} %fusion.21, f32[128,1536]{1,0:T(8,128)S(1)} %fusion.29, bf16[5,1536,768]{2,1,0:T(8,128)(2,1)} %param.6, bf16[1,128,768]{2,1,0:T(8,128)(2,1)} %rev.37), kind=kOutput, calls=%fused_computation.3 | convolution fusion | flops 302383104 | bytes 4915200 | tf_op jit(solution)/shard_map/dot_general | solution.py:61
  29.6 0.0 copy-start.2
  29.6 0.0 collective-permute-done.4
  29.6 2.7 %rev.41 = bf16[1,128,768]{2,1,0:T(8,128)(2,1)S(1)} reverse(bf16[1,128,768]{2,1,0:T(8,128)(2,1)} %collective-permute-done.4), dimensions={2} | reverse | bytes 393216 | tf_op jit(solution)/shard_map/rev | solution.py:22
  32.3 2.6 %fusion.7 = f32[128,1536]{1,0:T(8,128)S(1)} fusion(bf16[5,1536,768]{2,1,0:T(8,128)(2,1)} %param.6, bf16[1,128,768]{2,1,0:T(8,128)(2,1)S(1)} %rev.41), kind=kOutput, calls=%fused_computation.11 | convolution fusion | flops 301989888 | bytes 3342336 | tf_op jit(solution)/shard_map/dot_general | solution.py:61
  34.8 0.0 collective-permute-done.5
  34.9 2.7 %rev.40 = bf16[1,128,768]{2,1,0:T(8,128)(2,1)S(1)} reverse(bf16[1,128,768]{2,1,0:T(8,128)(2,1)} %collective-permute-done.5), dimensions={2} | reverse | bytes 393216 | tf_op jit(solution)/shard_map/rev | solution.py:22
  37.5 2.6 %fusion.6 = bf16[128,1536]{1,0:T(8,128)(2,1)S(1)} fusion(f32[128,1536]{1,0:T(8,128)S(1)} %fusion.7, f32[128,1536]{1,0:T(8,128)S(1)} %fusion.1, bf16[5,1536,768]{2,1,0:T(8,128)(2,1)} %param.6, bf16[1,128,768]{2,1,0:T(8,128)(2,1)S(1)} %rev.40), kind=kOutput, calls=%fused_computation.10 | convolution fusion | flops 302579712 | bytes 4521984 | tf_op jit(solution)/shard_map/dot_general | solution.py:61
  40.1 0.0 copy-start.4
  40.1 1.2 reverse.7
  41.3 2.7 %fusion.31 = f32[128,1536]{1,0:T(8,128)S(1)} fusion(bf16[5,1536,768]{2,1,0:T(8,128)(2,1)} %param.6, bf16[1,128,768]{2,1,0:T(8,128)(2,1)} %collective-permute-done.5), kind=kOutput, calls=%fused_computation.35 | convolution fusion | flops 301989888 | bytes 3342336 | tf_op jit(solution)/shard_map/dot_general | solution.py:61
  44.0 0.0 copy-done.2
  44.0 2.5 %fusion.9 = f32[128,1536]{1,0:T(8,128)S(1)} fusion(bf16[5,1536,768]{2,1,0:T(8,128)(2,1)} %param.6, bf16[1,128,768]{2,1,0:T(8,128)(2,1)S(1)} %copy-done.2), kind=kOutput, calls=%fused_computation.13 | convolution fusion | flops 301989888 | bytes 3342336 | tf_op jit(solution)/shard_map/dot_general | solution.py:61
  46.5 2.7 %fusion.4 = f32[128,1536]{1,0:T(8,128)S(1)} fusion(f32[128,1536]{1,0:T(8,128)S(1)} %fusion.23, f32[128,1536]{1,0:T(8,128)S(1)} %fusion.31, bf16[5,1536,768]{2,1,0:T(8,128)(2,1)} %param.6, bf16[1,128,768]{2,1,0:T(8,128)(2,1)} %collective-permute-done.4), kind=kOutput, calls=%fused_computation.8 | convolution fusion | flops 302383104 | bytes 4915200 | tf_op jit(solution)/shard_map/dot_general | solution.py:61
  49.3 0.0 copy-done
  49.3 0.0 copy-done.5
  49.3 0.0 copy-done.4
  49.3 3.1 %fusion.115 = (f32[1536]{0:T(1024)S(1)}, f32[128]{0:T(128)S(1)}, f32[1,128,1536]{2,1,0:T(8,128)S(1)}) fusion(bf16[1,128,1536]{2,1,0:T(8,128)(2,1)S(1)} %copy-done, f32[128]{0:T(128)S(1)} %add_rsqrt_fusion, f32[1536]{0:T(1024)S(1)} %copy-done.5, bf16[128,1536]{1,0:T(8,128)(2,1)S(1)} %reverse.7, f32[128,1536]{1,0:T(8,128)S(1)} %fusion.9, ...), kind=kOutput, calls=%fused_computation.99 | convolution fusion | flops 308083072 | bytes 5714944 | tf_op jit(solution)/shard_map/dot_general | solution.py:61
  52.4 1.3 fusion.114
  53.7 5.5 %collective-permute-start = (bf16[1,128,1536]{2,1,0:T(8,128)(2,1)S(1)}, bf16[1,128,1536]{2,1,0:T(8,128)(2,1)S(1)}, u32[]{:S(2)}, u32[]{:S(2)}) collective-permute-start(bf16[1,128,1536]{2,1,0:T(8,128)(2,1)S(1)} %get-tuple-element.6), channel_id=1, source_target_pairs={{0,4},{1,5},{2,6},{3,7},{4,8},{5,9},{6,10},{7,11},{8,12},{9,13},{1... | collective-permute-start | bytes 1179656 | tf_op jit(solution)/shard_map/ppermute | solution.py:14
  59.2 3.6 %collective-permute-start.1 = (bf16[1,128,1536]{2,1,0:T(8,128)(2,1)S(1)}, bf16[1,128,1536]{2,1,0:T(8,128)(2,1)S(1)}, u32[]{:S(2)}, u32[]{:S(2)}) collective-permute-start(bf16[1,128,1536]{2,1,0:T(8,128)(2,1)S(1)} %get-tuple-element.6), channel_id=1, source_target_pairs={{0,2},{1,3},{2,4},{3,5},{4,6},{5,7},{6,8},{7,9},{8,10},{9,11},{10,... | collective-permute-start | bytes 1179656 | tf_op jit(solution)/shard_map/ppermute | solution.py:14
  62.8 1.3 collective-permute-start.2
  64.1 1.3 collective-permute-start.3
  65.4 1.2 rev.34
  66.6 2.1 %fusion.27 = f32[128,768]{1,0:T(8,128)S(1)} fusion(bf16[5,1536,768]{2,1,0:T(8,128)(2,1)} %param.6, bf16[1,128,1536]{2,1,0:T(8,128)(2,1)S(1)} %get-tuple-element.6), kind=kOutput, calls=%fused_computation.31 | convolution fusion | flops 301989888 | bytes 3145728 | tf_op jit(solution)/shard_map/dot_general | solution.py:51
  68.8 47.5 %psum.7 = f32[1536]{0:T(1024)S(1)} all-reduce(f32[1536]{0:T(1024)S(1)} %get-tuple-element.3), channel_id=1, replica_groups=mesh['dp'=2,'ctx'=16] {'dp','ctx'}, use_global_device_ids=true, to_apply=%region_3.0 | all-reduce | flops 1536 | bytes 12288 | tf_op jit(solution)/shard_map/psum | solution.py:94
  116.3 2.1 %fusion.25 = f32[128,768]{1,0:T(8,128)S(1)} fusion(bf16[5,1536,768]{2,1,0:T(8,128)(2,1)} %param.6, bf16[1,128,1536]{2,1,0:T(8,128)(2,1)S(1)} %rev.34), kind=kOutput, calls=%fused_computation.29 | convolution fusion | flops 301989888 | bytes 3145728 | tf_op jit(solution)/shard_map/dot_general | solution.py:51
  118.5 0.6 broadcast_multiply_fusion
  119.1 0.0 collective-permute-done
  119.1 1.2 rev.36
  120.3 2.1 %fusion.11 = f32[128,768]{1,0:T(8,128)S(1)} fusion(bf16[5,1536,768]{2,1,0:T(8,128)(2,1)} %param.6, bf16[1,128,1536]{2,1,0:T(8,128)(2,1)S(1)} %rev.36), kind=kOutput, calls=%fused_computation.15 | convolution fusion | flops 301989888 | bytes 3145728 | tf_op jit(solution)/shard_map/dot_general | solution.py:51
  122.5 0.0 collective-permute-done.1
  122.5 1.2 rev.35
  123.7 2.1 %fusion.17 = f32[128,768]{1,0:T(8,128)S(1)} fusion(bf16[5,1536,768]{2,1,0:T(8,128)(2,1)} %param.6, bf16[1,128,1536]{2,1,0:T(8,128)(2,1)S(1)} %rev.35), kind=kOutput, calls=%fused_computation.21 | convolution fusion | flops 301989888 | bytes 3145728 | tf_op jit(solution)/shard_map/dot_general | solution.py:51
  125.8 0.0 collective-permute-done.2
  125.9 6.7 %rev.33 = bf16[1,128,1536]{2,1,0:T(8,128)(2,1)} reverse(bf16[1,128,1536]{2,1,0:T(8,128)(2,1)} %collective-permute-done.2), dimensions={2} | reverse | bytes 786432 | tf_op jit(solution)/shard_map/rev | solution.py:22
  132.6 2.3 %fusion.33 = f32[128,768]{1,0:T(8,128)S(1)} fusion(bf16[5,1536,768]{2,1,0:T(8,128)(2,1)} %param.6, bf16[1,128,1536]{2,1,0:T(8,128)(2,1)} %rev.33), kind=kOutput, calls=%fused_computation.37 | convolution fusion | flops 301989888 | bytes 3145728 | tf_op jit(solution)/shard_map/dot_general | solution.py:51
  134.8 0.0 collective-permute-done.3
  134.9 5.2 %rev.32 = bf16[1,128,1536]{2,1,0:T(8,128)(2,1)S(1)} reverse(bf16[1,128,1536]{2,1,0:T(8,128)(2,1)} %collective-permute-done.3), dimensions={2} | reverse | bytes 786432 | tf_op jit(solution)/shard_map/rev | solution.py:22
  140.1 2.2 %fusion.90 = bf16[128,768]{1,0:T(8,128)(2,1)S(1)} fusion(f32[128,768]{1,0:T(8,128)S(1)} %fusion.11, f32[128,768]{1,0:T(8,128)S(1)} %fusion.17, f32[128,768]{1,0:T(8,128)S(1)} %fusion.25, f32[128,768]{1,0:T(8,128)S(1)} %fusion.33, bf16[5,1536,768]{2,1,0:T(8,128)(2,1)} %param.6, bf16[1,128,1536]{2,1,0:T(8,128)(2,1)S(1)} %rev.32), kind=kOutput, calls=%fused_computation.76 | convolution fusion | flops 302481408 | bytes 4521984 | tf_op jit(solution)/shard_map/dot_general | solution.py:51
  142.2 0.6 reverse.6
  142.9 2.3 %fusion.13 = f32[128,768]{1,0:T(8,128)S(1)} fusion(bf16[5,1536,768]{2,1,0:T(8,128)(2,1)} %param.6, bf16[1,128,1536]{2,1,0:T(8,128)(2,1)} %collective-permute-done.3), kind=kOutput, calls=%fused_computation.17 | convolution fusion | flops 301989888 | bytes 3145728 | tf_op jit(solution)/shard_map/dot_general | solution.py:51
  145.2 2.3 %fusion.19 = f32[128,768]{1,0:T(8,128)S(1)} fusion(bf16[5,1536,768]{2,1,0:T(8,128)(2,1)} %param.6, bf16[1,128,1536]{2,1,0:T(8,128)(2,1)} %collective-permute-done.2), kind=kOutput, calls=%fused_computation.23 | convolution fusion | flops 301989888 | bytes 3145728 | tf_op jit(solution)/shard_map/dot_general | solution.py:51
  147.5 2.1 %fusion.35 = f32[128,768]{1,0:T(8,128)S(1)} fusion(bf16[5,1536,768]{2,1,0:T(8,128)(2,1)} %param.6, bf16[1,128,1536]{2,1,0:T(8,128)(2,1)S(1)} %collective-permute-done.1), kind=kOutput, calls=%fused_computation.39 | convolution fusion | flops 301989888 | bytes 3145728 | tf_op jit(solution)/shard_map/dot_general | solution.py:51
  149.6 2.9 %fusion.96 = bf16[1,128,768]{2,1,0:T(8,128)(2,1)} fusion(f32[128,768]{1,0:T(8,128)S(1)} %fusion.13, f32[128,768]{1,0:T(8,128)S(1)} %fusion.19, f32[128,768]{1,0:T(8,128)S(1)} %fusion.27, f32[128,768]{1,0:T(8,128)S(1)} %fusion.35, bf16[5,1536,768]{2,1,0:T(8,128)(2,1)} %param.6, bf16[1,128,1536]{2,1,0:T(8,128)(2,1)S(1)} %collective-permute-done, ...), kind=kOutput, calls=%fused_computation.78 | convolution fusion | flops 302678016 | bytes 4718592 | tf_op jit(solution)/shard_map/dot_general | solution.py:51
  (2 shorter events, 0.0 us)
Async XLA Ops:
  0.6 20.1 %collective-permute-start.6 = (bf16[1,128,768]{2,1,0:T(8,128)(2,1)}, bf16[1,128,768]{2,1,0:T(8,128)(2,1)S(1)}, u32[]{:S(2)}, u32[]{:S(2)}) collective-permute-start(bf16[1,128,768]{2,1,0:T(8,128)(2,1)} %param.7), channel_id=1, source_target_pairs={{0,2},{1,3},{2,4},{3,5},{4,6},{5,7},{6,8},{7,9},{8,10},{9,11},{10,... | collective-permute-start | bytes 589832 | tf_op jit(solution)/shard_map/ppermute | solution.py:14
  5.5 18.4 %collective-permute-start.7 = (bf16[1,128,768]{2,1,0:T(8,128)(2,1)}, bf16[1,128,768]{2,1,0:T(8,128)(2,1)S(1)}, u32[]{:S(2)}, u32[]{:S(2)}) collective-permute-start(bf16[1,128,768]{2,1,0:T(8,128)(2,1)} %param.7), channel_id=1, source_target_pairs={{0,4},{1,5},{2,6},{3,7},{4,8},{5,9},{6,10},{7,11},{8,12},{9,13},{1... | collective-permute-start | bytes 589832 | tf_op jit(solution)/shard_map/ppermute | solution.py:14
  9.0 20.5 %collective-permute-start.4 = (bf16[1,128,768]{2,1,0:T(8,128)(2,1)}, bf16[1,128,768]{2,1,0:T(8,128)(2,1)}, u32[]{:S(2)}, u32[]{:S(2)}) collective-permute-start(bf16[1,128,768]{2,1,0:T(8,128)(2,1)} %param.7), channel_id=1, source_target_pairs={{4,0},{5,1},{6,2},{7,3},{8,4},{9,5},{10,6},{11,7},{12,8},{13,9},{1... | collective-permute-start | bytes 589832 | tf_op jit(solution)/shard_map/ppermute | solution.py:14
  10.3 24.5 %collective-permute-start.5 = (bf16[1,128,768]{2,1,0:T(8,128)(2,1)}, bf16[1,128,768]{2,1,0:T(8,128)(2,1)}, u32[]{:S(2)}, u32[]{:S(2)}) collective-permute-start(bf16[1,128,768]{2,1,0:T(8,128)(2,1)} %param.7), channel_id=1, source_target_pairs={{2,0},{3,1},{4,2},{5,3},{6,4},{7,5},{8,6},{9,7},{10,8},{11,9},{12,... | collective-permute-start | bytes 589832 | tf_op jit(solution)/shard_map/ppermute | solution.py:14
  20.7 3.2 %copy-start.3 = (bf16[1,128,768]{2,1,0:T(8,128)(2,1)}, bf16[1,128,768]{2,1,0:T(8,128)(2,1)S(1)}, u32[]{:S(2)}) copy-start(bf16[1,128,768]{2,1,0:T(8,128)(2,1)S(1)} %collective-permute-done.6) | copy-start | bytes 589828
  23.9 0.7 copy-start.1
  26.8 22.4 %copy-start = (bf16[1,128,1536]{2,1,0:T(8,128)(2,1)S(1)}, bf16[1,128,1536]{2,1,0:T(8,128)(2,1)}, u32[]{:S(2)}) copy-start(bf16[1,128,1536]{2,1,0:T(8,128)(2,1)} %param.4) | copy-start | bytes 1179652
  26.8 22.4 %copy-start.5 = (f32[1536]{0:T(1024)S(1)}, f32[1536]{0:T(1024)}, u32[]{:S(2)}) copy-start(f32[1536]{0:T(1024)} %param.5) | copy-start | bytes 18436
  29.6 14.4 %copy-start.2 = (bf16[1,128,768]{2,1,0:T(8,128)(2,1)S(1)}, bf16[1,128,768]{2,1,0:T(8,128)(2,1)}, u32[]{:S(2)}) copy-start(bf16[1,128,768]{2,1,0:T(8,128)(2,1)} %copy-done.1) | copy-start | bytes 589828
  40.1 9.2 %copy-start.4 = (bf16[1,128,768]{2,1,0:T(8,128)(2,1)S(1)}, bf16[1,128,768]{2,1,0:T(8,128)(2,1)}, u32[]{:S(2)}) copy-start(bf16[1,128,768]{2,1,0:T(8,128)(2,1)} %copy-done.3) | copy-start | bytes 589828
  53.7 65.4 %collective-permute-start = (bf16[1,128,1536]{2,1,0:T(8,128)(2,1)S(1)}, bf16[1,128,1536]{2,1,0:T(8,128)(2,1)S(1)}, u32[]{:S(2)}, u32[]{:S(2)}) collective-permute-start(bf16[1,128,1536]{2,1,0:T(8,128)(2,1)S(1)} %get-tuple-element.6), channel_id=1, source_target_pairs={{0,4},{1,5},{2,6},{3,7},{4,8},{5,9},{6,10},{7,11},{8,12},{9,13},{1... | collective-permute-start | bytes 1179656 | tf_op jit(solution)/shard_map/ppermute | solution.py:14
  59.2 63.3 %collective-permute-start.1 = (bf16[1,128,1536]{2,1,0:T(8,128)(2,1)S(1)}, bf16[1,128,1536]{2,1,0:T(8,128)(2,1)S(1)}, u32[]{:S(2)}, u32[]{:S(2)}) collective-permute-start(bf16[1,128,1536]{2,1,0:T(8,128)(2,1)S(1)} %get-tuple-element.6), channel_id=1, source_target_pairs={{0,2},{1,3},{2,4},{3,5},{4,6},{5,7},{6,8},{7,9},{8,10},{9,11},{10,... | collective-permute-start | bytes 1179656 | tf_op jit(solution)/shard_map/ppermute | solution.py:14
  62.8 63.0 %collective-permute-start.2 = (bf16[1,128,1536]{2,1,0:T(8,128)(2,1)S(1)}, bf16[1,128,1536]{2,1,0:T(8,128)(2,1)}, u32[]{:S(2)}, u32[]{:S(2)}) collective-permute-start(bf16[1,128,1536]{2,1,0:T(8,128)(2,1)S(1)} %get-tuple-element.6), channel_id=1, source_target_pairs={{2,0},{3,1},{4,2},{5,3},{6,4},{7,5},{8,6},{9,7},{10,8},{11,9},{12,... | collective-permute-start | bytes 1179656 | tf_op jit(solution)/shard_map/ppermute | solution.py:14
  64.1 70.7 %collective-permute-start.3 = (bf16[1,128,1536]{2,1,0:T(8,128)(2,1)S(1)}, bf16[1,128,1536]{2,1,0:T(8,128)(2,1)}, u32[]{:S(2)}, u32[]{:S(2)}) collective-permute-start(bf16[1,128,1536]{2,1,0:T(8,128)(2,1)S(1)} %get-tuple-element.6), channel_id=1, source_target_pairs={{4,0},{5,1},{6,2},{7,3},{8,4},{9,5},{10,6},{11,7},{12,8},{13,9},{1... | collective-permute-start | bytes 1179656 | tf_op jit(solution)/shard_map/ppermute | solution.py:14
where the time goes:
time: 155 us; the launch traced here: 153 us
  matrix products  49.2 us (32%)
  blocking collectives  47.5 us (31%)
  local copies, waits for them, and re-layouts  28.9 us (19%)
  starting transfers between devices  22.7 us (15%)
  other arithmetic  3.03 us (2%)
    psum x1, blocking collectives, per_device(): summed = lax.psum(partial_sum, ('dp', 'ctx'))  47.5 us
    dot_general x10, matrix products, apply_backward(): lax.dot_general(flat_rows, weight[tap_index], (((1,), (1,)), ((), ())), p...  26.6 us
    rev x10, local copies, waits for them, and re-layouts, flip_channels(): return values[:, :, ::-1]  26.4 us
    ppermute x8, starting transfers between devices, shifted(): return lax.ppermute(block, axis, route)  22.7 us
    dot_general x10, matrix products, apply_forward(): jnp.dot(flat_rows, weight[tap_index], preferred_element_type=jnp.float32)  22.6 us
  transfers between devices with their start and end apart: 8, of which 0 were waited for; matrix products, arithmetic and copies ran while one was open for 29% of the time, Pallas kernels for 0%

commit v1 on v0

--- a/solution.py
+++ b/solution.py
@@ -91,7 +91,7 @@
     _, pullback = jax.vjp(activate, scaled)
     grad_scaled = pullback(grad_hidden)[0]
     partial_sum = jnp.sum(grad_scaled * normed, axis=(0, 1))
-    summed = lax.psum(partial_sum, ("dp", "ctx"))
+    summed = lax.psum(lax.psum(partial_sum, "dp"), "ctx")
     total_rows = features.shape[0] * features.shape[1] * lax.axis_size("dp") * lax.axis_size("ctx")
     gain_grad = summed / math.sqrt(total_rows)
     grad_normed = grad_scaled * gain

time: 155 us -> 147 us (0.948)
  blocking collectives: 47.5 us -> 39.7 us
    psum x1 -> x2, blocking collectives: 47.5 us -> 39.7 us  [per_device(): summed = lax.psum(lax.psum(partial_sum, 'dp'), 'ctx')]
  transfers between devices with their start and end apart: 8 -> 8, of which waited for: 0 -> 0; matrix products, arithmetic and copies ran while one was open for 29% -> 31% of each run, Pallas kernels for 0% -> 0%
where the time goes in v1:
time: 147 us; the launch traced here: 145 us
  matrix products  49.2 us (33%)
  blocking collectives  39.7 us (27%)
  local copies, waits for them, and re-layouts  28.9 us (20%)
  starting transfers between devices  22.7 us (15%)
  other arithmetic  3.03 us (2%)
    psum x2, blocking collectives, per_device(): summed = lax.psum(lax.psum(partial_sum, 'dp'), 'ctx')  39.7 us
    dot_general x10, matrix products, apply_backward(): lax.dot_general(flat_rows, weight[tap_index], (((1,), (1,)), ((), ())), p...  26.6 us
    rev x10, local copies, waits for them, and re-layouts, flip_channels(): return values[:, :, ::-1]  26.4 us
    ppermute x8, starting transfers between devices, shifted(): return lax.ppermute(block, axis, route)  22.7 us
    dot_general x10, matrix products, apply_forward(): jnp.dot(flat_rows, weight[tap_index], preferred_element_type=jnp.float32)  22.6 us
  transfers between devices with their start and end apart: 8, of which 0 were waited for; matrix products, arithmetic and copies ran while one was open for 31% of the time, Pallas kernels for 0%

profile of v1, /device:TPU:0, one launch (start us, length us, event | category | flops | bytes accessed | tf_op | source)
XLA Modules:
  0.0 144.7 jit_solution(13048756174272062120)
XLA Ops:
  0.6 4.9 %collective-permute-start.6 = (bf16[1,128,768]{2,1,0:T(8,128)(2,1)}, bf16[1,128,768]{2,1,0:T(8,128)(2,1)S(1)}, u32[]{:S(2)}, u32[]{:S(2)}) collective-permute-start(bf16[1,128,768]{2,1,0:T(8,128)(2,1)} %param.7), channel_id=1, source_target_pairs={{0,2},{1,3},{2,4},{3,5},{4,6},{5,7},{6,8},{7,9},{8,10},{9,11},{10,... | collective-permute-start | bytes 589832 | tf_op jit(solution)/shard_map/ppermute | solution.py:14
  5.5 3.5 %collective-permute-start.7 = (bf16[1,128,768]{2,1,0:T(8,128)(2,1)}, bf16[1,128,768]{2,1,0:T(8,128)(2,1)S(1)}, u32[]{:S(2)}, u32[]{:S(2)}) collective-permute-start(bf16[1,128,768]{2,1,0:T(8,128)(2,1)} %param.7), channel_id=1, source_target_pairs={{0,4},{1,5},{2,6},{3,7},{4,8},{5,9},{6,10},{7,11},{8,12},{9,13},{1... | collective-permute-start | bytes 589832 | tf_op jit(solution)/shard_map/ppermute | solution.py:14
  9.0 1.3 collective-permute-start.4
  10.3 1.3 collective-permute-start.5
  11.6 2.7 %rev.39 = bf16[1,128,768]{2,1,0:T(8,128)(2,1)S(1)} reverse(bf16[1,128,768]{2,1,0:T(8,128)(2,1)} %param.7), dimensions={2} | reverse | bytes 393216 | tf_op jit(solution)/shard_map/rev | solution.py:22
  14.3 2.7 %fusion.23 = f32[128,1536]{1,0:T(8,128)S(1)} fusion(bf16[5,1536,768]{2,1,0:T(8,128)(2,1)} %param.6, bf16[1,128,768]{2,1,0:T(8,128)(2,1)} %param.7), kind=kOutput, calls=%fused_computation.27 | convolution fusion | flops 301989888 | bytes 3342336 | tf_op jit(solution)/shard_map/dot_general | solution.py:61
  17.0 2.6 %fusion.21 = f32[128,1536]{1,0:T(8,128)S(1)} fusion(bf16[5,1536,768]{2,1,0:T(8,128)(2,1)} %param.6, bf16[1,128,768]{2,1,0:T(8,128)(2,1)S(1)} %rev.39), kind=kOutput, calls=%fused_computation.25 | convolution fusion | flops 301989888 | bytes 3342336 | tf_op jit(solution)/shard_map/dot_general | solution.py:61
  19.5 1.2 fusion.116
  20.7 0.0 collective-permute-done.6
  20.7 0.0 copy-start.3
  20.7 0.6 rev.38
  21.4 2.5 %fusion.29 = f32[128,1536]{1,0:T(8,128)S(1)} fusion(bf16[5,1536,768]{2,1,0:T(8,128)(2,1)} %param.6, bf16[1,128,768]{2,1,0:T(8,128)(2,1)S(1)} %rev.38), kind=kOutput, calls=%fused_computation.33 | convolution fusion | flops 301989888 | bytes 3342336 | tf_op jit(solution)/shard_map/dot_general | solution.py:61
  23.9 0.0 collective-permute-done.7
  23.9 0.0 copy-done.3
  23.9 0.0 copy-start.1
  24.0 0.7 copy-done.1
  24.6 2.2 %rev.37 = bf16[1,128,768]{2,1,0:T(8,128)(2,1)} reverse(bf16[1,128,768]{2,1,0:T(8,128)(2,1)S(1)} %collective-permute-done.7), dimensions={2} | reverse | bytes 393216 | tf_op jit(solution)/shard_map/rev | solution.py:22
  26.8 0.0 copy-start
  26.8 2.7 %fusion.1 = f32[128,1536]{1,0:T(8,128)S(1)} fusion(f32[128,1536]{1,0:T(8,128)S(1)} %fusion.21, f32[128,1536]{1,0:T(8,128)S(1)} %fusion.29, bf16[5,1536,768]{2,1,0:T(8,128)(2,1)} %param.6, bf16[1,128,768]{2,1,0:T(8,128)(2,1)} %rev.37), kind=kOutput, calls=%fused_computation.3 | convolution fusion | flops 302383104 | bytes 4915200 | tf_op jit(solution)/shard_map/dot_general | solution.py:61
  29.6 0.0 copy-start.2
  29.6 0.0 collective-permute-done.4
  29.6 2.7 %rev.41 = bf16[1,128,768]{2,1,0:T(8,128)(2,1)S(1)} reverse(bf16[1,128,768]{2,1,0:T(8,128)(2,1)} %collective-permute-done.4), dimensions={2} | reverse | bytes 393216 | tf_op jit(solution)/shard_map/rev | solution.py:22
  32.3 2.6 %fusion.7 = f32[128,1536]{1,0:T(8,128)S(1)} fusion(bf16[5,1536,768]{2,1,0:T(8,128)(2,1)} %param.6, bf16[1,128,768]{2,1,0:T(8,128)(2,1)S(1)} %rev.41), kind=kOutput, calls=%fused_computation.11 | convolution fusion | flops 301989888 | bytes 3342336 | tf_op jit(solution)/shard_map/dot_general | solution.py:61
  34.8 0.0 collective-permute-done.5
  34.9 2.7 %rev.40 = bf16[1,128,768]{2,1,0:T(8,128)(2,1)S(1)} reverse(bf16[1,128,768]{2,1,0:T(8,128)(2,1)} %collective-permute-done.5), dimensions={2} | reverse | bytes 393216 | tf_op jit(solution)/shard_map/rev | solution.py:22
  37.5 2.6 %fusion.6 = bf16[128,1536]{1,0:T(8,128)(2,1)S(1)} fusion(f32[128,1536]{1,0:T(8,128)S(1)} %fusion.7, f32[128,1536]{1,0:T(8,128)S(1)} %fusion.1, bf16[5,1536,768]{2,1,0:T(8,128)(2,1)} %param.6, bf16[1,128,768]{2,1,0:T(8,128)(2,1)S(1)} %rev.40), kind=kOutput, calls=%fused_computation.10 | convolution fusion | flops 302579712 | bytes 4521984 | tf_op jit(solution)/shard_map/dot_general | solution.py:61
  40.1 0.0 copy-start.4
  40.1 1.2 reverse.7
  41.3 2.7 %fusion.31 = f32[128,1536]{1,0:T(8,128)S(1)} fusion(bf16[5,1536,768]{2,1,0:T(8,128)(2,1)} %param.6, bf16[1,128,768]{2,1,0:T(8,128)(2,1)} %collective-permute-done.5), kind=kOutput, calls=%fused_computation.35 | convolution fusion | flops 301989888 | bytes 3342336 | tf_op jit(solution)/shard_map/dot_general | solution.py:61
  44.0 0.0 copy-done.2
  44.0 2.5 %fusion.9 = f32[128,1536]{1,0:T(8,128)S(1)} fusion(bf16[5,1536,768]{2,1,0:T(8,128)(2,1)} %param.6, bf16[1,128,768]{2,1,0:T(8,128)(2,1)S(1)} %copy-done.2), kind=kOutput, calls=%fused_computation.13 | convolution fusion | flops 301989888 | bytes 3342336 | tf_op jit(solution)/shard_map/dot_general | solution.py:61
  46.5 2.7 %fusion.4 = f32[128,1536]{1,0:T(8,128)S(1)} fusion(f32[128,1536]{1,0:T(8,128)S(1)} %fusion.23, f32[128,1536]{1,0:T(8,128)S(1)} %fusion.31, bf16[5,1536,768]{2,1,0:T(8,128)(2,1)} %param.6, bf16[1,128,768]{2,1,0:T(8,128)(2,1)} %collective-permute-done.4), kind=kOutput, calls=%fused_computation.8 | convolution fusion | flops 302383104 | bytes 4915200 | tf_op jit(solution)/shard_map/dot_general | solution.py:61
  49.3 0.0 copy-done
  49.3 0.0 copy-done.5
  49.3 0.0 copy-done.4
  49.3 3.1 %fusion.115 = (f32[1536]{0:T(1024)S(1)}, f32[128]{0:T(128)S(1)}, f32[1,128,1536]{2,1,0:T(8,128)S(1)}) fusion(bf16[1,128,1536]{2,1,0:T(8,128)(2,1)S(1)} %copy-done, f32[128]{0:T(128)S(1)} %add_rsqrt_fusion, f32[1536]{0:T(1024)S(1)} %copy-done.5, bf16[128,1536]{1,0:T(8,128)(2,1)S(1)} %reverse.7, f32[128,1536]{1,0:T(8,128)S(1)} %fusion.9, ...), kind=kOutput, calls=%fused_computation.99 | convolution fusion | flops 308083072 | bytes 5714944 | tf_op jit(solution)/shard_map/dot_general | solution.py:61
  52.4 1.3 fusion.114
  53.7 5.5 %collective-permute-start = (bf16[1,128,1536]{2,1,0:T(8,128)(2,1)S(1)}, bf16[1,128,1536]{2,1,0:T(8,128)(2,1)S(1)}, u32[]{:S(2)}, u32[]{:S(2)}) collective-permute-start(bf16[1,128,1536]{2,1,0:T(8,128)(2,1)S(1)} %get-tuple-element.6), channel_id=1, source_target_pairs={{0,4},{1,5},{2,6},{3,7},{4,8},{5,9},{6,10},{7,11},{8,12},{9,13},{1... | collective-permute-start | bytes 1179656 | tf_op jit(solution)/shard_map/ppermute | solution.py:14
  59.2 3.6 %collective-permute-start.1 = (bf16[1,128,1536]{2,1,0:T(8,128)(2,1)S(1)}, bf16[1,128,1536]{2,1,0:T(8,128)(2,1)S(1)}, u32[]{:S(2)}, u32[]{:S(2)}) collective-permute-start(bf16[1,128,1536]{2,1,0:T(8,128)(2,1)S(1)} %get-tuple-element.6), channel_id=1, source_target_pairs={{0,2},{1,3},{2,4},{3,5},{4,6},{5,7},{6,8},{7,9},{8,10},{9,11},{10,... | collective-permute-start | bytes 1179656 | tf_op jit(solution)/shard_map/ppermute | solution.py:14
  62.8 1.3 collective-permute-start.2
  64.1 1.3 collective-permute-start.3
  65.4 1.2 rev.34
  66.6 2.1 %fusion.27 = f32[128,768]{1,0:T(8,128)S(1)} fusion(bf16[5,1536,768]{2,1,0:T(8,128)(2,1)} %param.6, bf16[1,128,1536]{2,1,0:T(8,128)(2,1)S(1)} %get-tuple-element.6), kind=kOutput, calls=%fused_computation.31 | convolution fusion | flops 301989888 | bytes 3145728 | tf_op jit(solution)/shard_map/dot_general | solution.py:51
  68.8 5.0 %psum.14 = f32[1536]{0:T(1024)S(1)} all-reduce(f32[1536]{0:T(1024)S(1)} %get-tuple-element.3), channel_id=1, replica_groups=mesh['dp'=2,'ctx'=16] {'dp'}, use_global_device_ids=true, to_apply=%region_3.0 | all-reduce | flops 1536 | bytes 12288 | tf_op jit(solution)/shard_map/psum | solution.py:94
  73.8 34.7 %psum.15 = f32[1536]{0:T(1024)S(1)} all-reduce(f32[1536]{0:T(1024)S(1)} %psum.14), channel_id=1, replica_groups=mesh['dp'=2,'ctx'=16] {'ctx'}, use_global_device_ids=true, to_apply=%region_4.0 | all-reduce | flops 1536 | bytes 12288 | tf_op jit(solution)/shard_map/psum | solution.py:94
  108.5 2.1 %fusion.25 = f32[128,768]{1,0:T(8,128)S(1)} fusion(bf16[5,1536,768]{2,1,0:T(8,128)(2,1)} %param.6, bf16[1,128,1536]{2,1,0:T(8,128)(2,1)S(1)} %rev.34), kind=kOutput, calls=%fused_computation.29 | convolution fusion | flops 301989888 | bytes 3145728 | tf_op jit(solution)/shard_map/dot_general | solution.py:51
  110.7 0.6 broadcast_multiply_fusion
  111.3 0.0 collective-permute-done
  111.3 1.2 rev.36
  112.5 2.1 %fusion.11 = f32[128,768]{1,0:T(8,128)S(1)} fusion(bf16[5,1536,768]{2,1,0:T(8,128)(2,1)} %param.6, bf16[1,128,1536]{2,1,0:T(8,128)(2,1)S(1)} %rev.36), kind=kOutput, calls=%fused_computation.15 | convolution fusion | flops 301989888 | bytes 3145728 | tf_op jit(solution)/shard_map/dot_general | solution.py:51
  114.7 0.0 collective-permute-done.1
  114.7 1.2 rev.35
  115.9 2.1 %fusion.17 = f32[128,768]{1,0:T(8,128)S(1)} fusion(bf16[5,1536,768]{2,1,0:T(8,128)(2,1)} %param.6, bf16[1,128,1536]{2,1,0:T(8,128)(2,1)S(1)} %rev.35), kind=kOutput, calls=%fused_computation.21 | convolution fusion | flops 301989888 | bytes 3145728 | tf_op jit(solution)/shard_map/dot_general | solution.py:51
  118.1 0.0 collective-permute-done.2
  118.1 6.7 %rev.33 = bf16[1,128,1536]{2,1,0:T(8,128)(2,1)} reverse(bf16[1,128,1536]{2,1,0:T(8,128)(2,1)} %collective-permute-done.2), dimensions={2} | reverse | bytes 786432 | tf_op jit(solution)/shard_map/rev | solution.py:22
  124.8 2.3 %fusion.33 = f32[128,768]{1,0:T(8,128)S(1)} fusion(bf16[5,1536,768]{2,1,0:T(8,128)(2,1)} %param.6, bf16[1,128,1536]{2,1,0:T(8,128)(2,1)} %rev.33), kind=kOutput, calls=%fused_computation.37 | convolution fusion | flops 301989888 | bytes 3145728 | tf_op jit(solution)/shard_map/dot_general | solution.py:51
  127.0 0.0 collective-permute-done.3
  127.1 5.2 %rev.32 = bf16[1,128,1536]{2,1,0:T(8,128)(2,1)S(1)} reverse(bf16[1,128,1536]{2,1,0:T(8,128)(2,1)} %collective-permute-done.3), dimensions={2} | reverse | bytes 786432 | tf_op jit(solution)/shard_map/rev | solution.py:22
  132.3 2.2 %fusion.90 = bf16[128,768]{1,0:T(8,128)(2,1)S(1)} fusion(f32[128,768]{1,0:T(8,128)S(1)} %fusion.11, f32[128,768]{1,0:T(8,128)S(1)} %fusion.17, f32[128,768]{1,0:T(8,128)S(1)} %fusion.25, f32[128,768]{1,0:T(8,128)S(1)} %fusion.33, bf16[5,1536,768]{2,1,0:T(8,128)(2,1)} %param.6, bf16[1,128,1536]{2,1,0:T(8,128)(2,1)S(1)} %rev.32), kind=kOutput, calls=%fused_computation.76 | convolution fusion | flops 302481408 | bytes 4521984 | tf_op jit(solution)/shard_map/dot_general | solution.py:51
  134.4 0.6 reverse.6
  135.1 2.3 %fusion.13 = f32[128,768]{1,0:T(8,128)S(1)} fusion(bf16[5,1536,768]{2,1,0:T(8,128)(2,1)} %param.6, bf16[1,128,1536]{2,1,0:T(8,128)(2,1)} %collective-permute-done.3), kind=kOutput, calls=%fused_computation.17 | convolution fusion | flops 301989888 | bytes 3145728 | tf_op jit(solution)/shard_map/dot_general | solution.py:51
  137.4 2.3 %fusion.19 = f32[128,768]{1,0:T(8,128)S(1)} fusion(bf16[5,1536,768]{2,1,0:T(8,128)(2,1)} %param.6, bf16[1,128,1536]{2,1,0:T(8,128)(2,1)} %collective-permute-done.2), kind=kOutput, calls=%fused_computation.23 | convolution fusion | flops 301989888 | bytes 3145728 | tf_op jit(solution)/shard_map/dot_general | solution.py:51
  139.7 2.1 %fusion.35 = f32[128,768]{1,0:T(8,128)S(1)} fusion(bf16[5,1536,768]{2,1,0:T(8,128)(2,1)} %param.6, bf16[1,128,1536]{2,1,0:T(8,128)(2,1)S(1)} %collective-permute-done.1), kind=kOutput, calls=%fused_computation.39 | convolution fusion | flops 301989888 | bytes 3145728 | tf_op jit(solution)/shard_map/dot_general | solution.py:51
  141.8 2.9 %fusion.96 = bf16[1,128,768]{2,1,0:T(8,128)(2,1)} fusion(f32[128,768]{1,0:T(8,128)S(1)} %fusion.13, f32[128,768]{1,0:T(8,128)S(1)} %fusion.19, f32[128,768]{1,0:T(8,128)S(1)} %fusion.27, f32[128,768]{1,0:T(8,128)S(1)} %fusion.35, bf16[5,1536,768]{2,1,0:T(8,128)(2,1)} %param.6, bf16[1,128,1536]{2,1,0:T(8,128)(2,1)S(1)} %collective-permute-done, ...), kind=kOutput, calls=%fused_computation.78 | convolution fusion | flops 302678016 | bytes 4718592 | tf_op jit(solution)/shard_map/dot_general | solution.py:51
  (3 shorter events, 0.0 us)
Async XLA Ops:
  0.6 20.1 %collective-permute-start.6 = (bf16[1,128,768]{2,1,0:T(8,128)(2,1)}, bf16[1,128,768]{2,1,0:T(8,128)(2,1)S(1)}, u32[]{:S(2)}, u32[]{:S(2)}) collective-permute-start(bf16[1,128,768]{2,1,0:T(8,128)(2,1)} %param.7), channel_id=1, source_target_pairs={{0,2},{1,3},{2,4},{3,5},{4,6},{5,7},{6,8},{7,9},{8,10},{9,11},{10,... | collective-permute-start | bytes 589832 | tf_op jit(solution)/shard_map/ppermute | solution.py:14
  5.5 18.4 %collective-permute-start.7 = (bf16[1,128,768]{2,1,0:T(8,128)(2,1)}, bf16[1,128,768]{2,1,0:T(8,128)(2,1)S(1)}, u32[]{:S(2)}, u32[]{:S(2)}) collective-permute-start(bf16[1,128,768]{2,1,0:T(8,128)(2,1)} %param.7), channel_id=1, source_target_pairs={{0,4},{1,5},{2,6},{3,7},{4,8},{5,9},{6,10},{7,11},{8,12},{9,13},{1... | collective-permute-start | bytes 589832 | tf_op jit(solution)/shard_map/ppermute | solution.py:14
  9.0 20.5 %collective-permute-start.4 = (bf16[1,128,768]{2,1,0:T(8,128)(2,1)}, bf16[1,128,768]{2,1,0:T(8,128)(2,1)}, u32[]{:S(2)}, u32[]{:S(2)}) collective-permute-start(bf16[1,128,768]{2,1,0:T(8,128)(2,1)} %param.7), channel_id=1, source_target_pairs={{4,0},{5,1},{6,2},{7,3},{8,4},{9,5},{10,6},{11,7},{12,8},{13,9},{1... | collective-permute-start | bytes 589832 | tf_op jit(solution)/shard_map/ppermute | solution.py:14
  10.3 24.5 %collective-permute-start.5 = (bf16[1,128,768]{2,1,0:T(8,128)(2,1)}, bf16[1,128,768]{2,1,0:T(8,128)(2,1)}, u32[]{:S(2)}, u32[]{:S(2)}) collective-permute-start(bf16[1,128,768]{2,1,0:T(8,128)(2,1)} %param.7), channel_id=1, source_target_pairs={{2,0},{3,1},{4,2},{5,3},{6,4},{7,5},{8,6},{9,7},{10,8},{11,9},{12,... | collective-permute-start | bytes 589832 | tf_op jit(solution)/shard_map/ppermute | solution.py:14
  20.7 3.2 %copy-start.3 = (bf16[1,128,768]{2,1,0:T(8,128)(2,1)}, bf16[1,128,768]{2,1,0:T(8,128)(2,1)S(1)}, u32[]{:S(2)}) copy-start(bf16[1,128,768]{2,1,0:T(8,128)(2,1)S(1)} %collective-permute-done.6) | copy-start | bytes 589828
  23.9 0.7 copy-start.1
  26.8 22.4 %copy-start = (bf16[1,128,1536]{2,1,0:T(8,128)(2,1)S(1)}, bf16[1,128,1536]{2,1,0:T(8,128)(2,1)}, u32[]{:S(2)}) copy-start(bf16[1,128,1536]{2,1,0:T(8,128)(2,1)} %param.4) | copy-start | bytes 1179652
  26.8 22.4 %copy-start.5 = (f32[1536]{0:T(1024)S(1)}, f32[1536]{0:T(1024)}, u32[]{:S(2)}) copy-start(f32[1536]{0:T(1024)} %param.5) | copy-start | bytes 18436
  29.6 14.4 %copy-start.2 = (bf16[1,128,768]{2,1,0:T(8,128)(2,1)S(1)}, bf16[1,128,768]{2,1,0:T(8,128)(2,1)}, u32[]{:S(2)}) copy-start(bf16[1,128,768]{2,1,0:T(8,128)(2,1)} %copy-done.1) | copy-start | bytes 589828
  40.1 9.2 %copy-start.4 = (bf16[1,128,768]{2,1,0:T(8,128)(2,1)S(1)}, bf16[1,128,768]{2,1,0:T(8,128)(2,1)}, u32[]{:S(2)}) copy-start(bf16[1,128,768]{2,1,0:T(8,128)(2,1)} %copy-done.3) | copy-start | bytes 589828
  53.7 57.6 %collective-permute-start = (bf16[1,128,1536]{2,1,0:T(8,128)(2,1)S(1)}, bf16[1,128,1536]{2,1,0:T(8,128)(2,1)S(1)}, u32[]{:S(2)}, u32[]{:S(2)}) collective-permute-start(bf16[1,128,1536]{2,1,0:T(8,128)(2,1)S(1)} %get-tuple-element.6), channel_id=1, source_target_pairs={{0,4},{1,5},{2,6},{3,7},{4,8},{5,9},{6,10},{7,11},{8,12},{9,13},{1... | collective-permute-start | bytes 1179656 | tf_op jit(solution)/shard_map/ppermute | solution.py:14
  59.2 55.5 %collective-permute-start.1 = (bf16[1,128,1536]{2,1,0:T(8,128)(2,1)S(1)}, bf16[1,128,1536]{2,1,0:T(8,128)(2,1)S(1)}, u32[]{:S(2)}, u32[]{:S(2)}) collective-permute-start(bf16[1,128,1536]{2,1,0:T(8,128)(2,1)S(1)} %get-tuple-element.6), channel_id=1, source_target_pairs={{0,2},{1,3},{2,4},{3,5},{4,6},{5,7},{6,8},{7,9},{8,10},{9,11},{10,... | collective-permute-start | bytes 1179656 | tf_op jit(solution)/shard_map/ppermute | solution.py:14
  62.8 55.2 %collective-permute-start.2 = (bf16[1,128,1536]{2,1,0:T(8,128)(2,1)S(1)}, bf16[1,128,1536]{2,1,0:T(8,128)(2,1)}, u32[]{:S(2)}, u32[]{:S(2)}) collective-permute-start(bf16[1,128,1536]{2,1,0:T(8,128)(2,1)S(1)} %get-tuple-element.6), channel_id=1, source_target_pairs={{2,0},{3,1},{4,2},{5,3},{6,4},{7,5},{8,6},{9,7},{10,8},{11,9},{12,... | collective-permute-start | bytes 1179656 | tf_op jit(solution)/shard_map/ppermute | solution.py:14
  64.1 62.9 %collective-permute-start.3 = (bf16[1,128,1536]{2,1,0:T(8,128)(2,1)S(1)}, bf16[1,128,1536]{2,1,0:T(8,128)(2,1)}, u32[]{:S(2)}, u32[]{:S(2)}) collective-permute-start(bf16[1,128,1536]{2,1,0:T(8,128)(2,1)S(1)} %get-tuple-element.6), channel_id=1, source_target_pairs={{4,0},{5,1},{6,2},{7,3},{8,4},{9,5},{10,6},{11,7},{12,8},{13,9},{1... | collective-permute-start | bytes 1179656 | tf_op jit(solution)/shard_map/ppermute | solution.py:14
